TPU v7x, 32 devices: a whole 2x2x4 slice. The times are simulated.
32 devices in a mesh: pages: 2 (over y), tile: 8 (over z, x), mp: 2 (over core).
Axes of the slice: x: 2, y: 2, z: 4, core: 2. Of those that a mesh axis runs over, the one named last changes fastest.
Arguments:
- queries: bfloat16 [3072, 1024], P(('pages', 'tile'), 'mp'), parts along dimension 0, may hold values from -10.5 to 10.5
- key_rows: bfloat16 [3072, 1024], P(('pages', 'tile'), 'mp'), parts along dimension 0, may hold values from -8.5 to 8.5
- value_rows: bfloat16 [3072, 1024], P(('pages', 'tile'), 'mp'), parts along dimension 0, may hold values from -6 to 6
- grad_out: bfloat16 [3072, 1024], P(('pages', 'tile'), 'mp'), parts along dimension 0, may hold values from -6 to 6
- owner_shard: int32 [3072], P(('pages', 'tile')), parts along dimension 0, may hold values from 0 to 7, as said below
- logit_scale: float32 [16], P('mp'), may hold values from 0.5 to 2
Outputs:
- grad_queries: bfloat16 [3072, 1024], P(('pages', 'tile'), 'mp'), parts along dimension 0
- grad_keys: bfloat16 [3072, 1024], P(('pages', 'tile'), 'mp'), parts along dimension 0
- grad_values: bfloat16 [3072, 1024], P(('pages', 'tile'), 'mp'), parts along dimension 0
There are 2 independent parts, one for each index of `pages`. A program takes and returns all parts, laid end to end along the dimension named above; an argument that names none is the same for every part. Nothing has to cross between parts.
Inputs may be any that keep to these rules, and one draw needn't show every extreme that they name: `owner_shard`: the 192 tokens of one index of tile name any one region at most 48 times; in every draw one region is named exactly 48 times by the tokens of every index of tile, so it holds 384 tokens.
All inputs are finite; a program needn't handle non-finite values.
Results may differ from a plain program's by a relative error of at most 0.0035.
The roundings to bfloat16 on the way count: a program that leaves them out, or rounds other values in their place, can miss the bound.
Values may be sent and summed in bfloat16 or wider, within the bound.
A program may use at most 64 MiB of HBM per device.

v0:
```python
import math

import jax
import jax.numpy as jnp
from jax import lax
from jax.sharding import PartitionSpec as P


def attend_heads(query_heads, key_heads, value_heads, dout_heads, live_rows):
    pair_mask = live_rows[None, :, None] & live_rows[None, None, :]
    scores = jnp.einsum("ihe,jhe->hij", query_heads, key_heads, preferred_element_type=jnp.float32)
    scores = jnp.where(pair_mask, scores, -1e30)
    row_max = jnp.max(scores, axis=2, keepdims=True)
    raw_weights = jnp.where(pair_mask, jnp.exp(scores - row_max), 0.0)
    row_sum = jnp.sum(raw_weights, axis=2, keepdims=True)
    row_sum = jnp.where(live_rows[None, :, None], row_sum, 1.0)
    weights = raw_weights / row_sum
    weights_low = weights.astype(jnp.bfloat16)
    attended = jnp.einsum(
        "hij,jhe->ihe", weights_low, value_heads, preferred_element_type=jnp.float32
    )
    row_delta = jnp.sum(dout_heads.astype(jnp.float32) * attended, axis=2)
    dprobs = jnp.einsum("ihe,jhe->hij", dout_heads, value_heads, preferred_element_type=jnp.float32)
    dscores = (weights * (dprobs - jnp.transpose(row_delta)[:, :, None])).astype(jnp.bfloat16)
    grad_value = jnp.einsum(
        "hij,ihe->jhe", weights_low, dout_heads, preferred_element_type=jnp.float32
    ).astype(jnp.bfloat16)
    grad_key = jnp.einsum(
        "hij,ihe->jhe", dscores, query_heads, preferred_element_type=jnp.float32
    ).astype(jnp.bfloat16)
    grad_raw = jnp.einsum(
        "hij,jhe->ihe", dscores, key_heads, preferred_element_type=jnp.float32
    ).astype(jnp.bfloat16)
    return (grad_raw, grad_key, grad_value)


def attend_items(query_items, key_items, value_items, dout_items, live_rows):
    capacity = query_items.shape[0]
    item_count = query_items.shape[1]
    head_size = query_items.shape[2] // 2
    outputs = ([], [], [])
    for item_index in range(item_count):
        halves = ([], [], [])
        for half_index in range(2):
            lower = half_index * head_size
            upper = lower + head_size
            pieces = attend_heads(
                query_items[:, item_index, lower:upper].reshape(capacity, 1, head_size),
                key_items[:, item_index, lower:upper].reshape(capacity, 1, head_size),
                value_items[:, item_index, lower:upper].reshape(capacity, 1, head_size),
                dout_items[:, item_index, lower:upper].reshape(capacity, 1, head_size),
                live_rows,
            )
            for holder, piece in zip(halves, pieces):
                holder.append(piece.reshape(capacity, head_size))
        for holder, parts_list in zip(outputs, halves):
            holder.append(jnp.concatenate(parts_list, axis=1))
    return tuple((jnp.stack(holder, axis=1) for holder in outputs))


def slot_places(owner_shard, shards, slot):
    one_hot = (owner_shard[:, None] == jnp.arange(shards, dtype=jnp.int32)[None, :]).astype(
        jnp.int32
    )
    before = jnp.cumsum(one_hot, axis=0) - one_hot
    rank = jnp.sum(before * one_hot, axis=1)
    return owner_shard * slot + rank


def local(queries, key_rows, value_rows, grad_out, owner_shard, logit_scale):
    shards = lax.axis_size("tile")
    tok_rows, columns = queries.shape
    heads_here = logit_scale.shape[0]
    head_size = columns // heads_here
    capacity = 2 * tok_rows
    slot = capacity // shards
    pairs = heads_here // 2
    width = 2 * head_size
    slot_index = slot_places(owner_shard, shards, slot)
    scale_cols = jnp.repeat(logit_scale / math.sqrt(head_size), head_size)
    scaled = (queries.astype(jnp.float32) * scale_cols).astype(jnp.bfloat16)

    def spread(source):
        return jnp.zeros((capacity,) + source.shape[1:], source.dtype).at[slot_index].set(source)

    sent_query = spread(scaled)
    sent_key = spread(key_rows)
    sent_value = spread(value_rows)
    sent_dout = spread(grad_out)
    flags = spread(jnp.ones((tok_rows,), jnp.int32))
    got_query, got_key, got_value, got_dout, got_flags = (
        lax.all_to_all(sent_query, "tile", split_axis=0, concat_axis=0, tiled=True),
        lax.all_to_all(sent_key, "tile", split_axis=0, concat_axis=0, tiled=True),
        lax.all_to_all(sent_value, "tile", split_axis=0, concat_axis=0, tiled=True),
        lax.all_to_all(sent_dout, "tile", split_axis=0, concat_axis=0, tiled=True),
        lax.all_to_all(flags, "tile", split_axis=0, concat_axis=0, tiled=True),
    )
    grad_raw, grad_key, grad_value = attend_items(
        got_query.reshape(capacity, pairs, width),
        got_key.reshape(capacity, pairs, width),
        got_value.reshape(capacity, pairs, width),
        got_dout.reshape(capacity, pairs, width),
        got_flags > 0,
    )
    returned = (
        lax.all_to_all(
            grad_raw.reshape(capacity, columns), "tile", split_axis=0, concat_axis=0, tiled=True
        ),
        lax.all_to_all(
            grad_key.reshape(capacity, columns), "tile", split_axis=0, concat_axis=0, tiled=True
        ),
        lax.all_to_all(
            grad_value.reshape(capacity, columns), "tile", split_axis=0, concat_axis=0, tiled=True
        ),
    )
    grad_queries = (returned[0][slot_index].astype(jnp.float32) * scale_cols).astype(jnp.bfloat16)
    return (grad_queries, returned[1][slot_index], returned[2][slot_index])


def solution(mesh):
    return jax.shard_map(
        local,
        mesh=mesh,
        in_specs=(
            P(("pages", "tile"), "mp"),
            P(("pages", "tile"), "mp"),
            P(("pages", "tile"), "mp"),
            P(("pages", "tile"), "mp"),
            P(("pages", "tile")),
            P("mp"),
        ),
        out_specs=(
            P(("pages", "tile"), "mp"),
            P(("pages", "tile"), "mp"),
            P(("pages", "tile"), "mp"),
        ),
        check_vma=False,
    )
```

profile of v0, /device:TPU:0, one launch (start us, length us, event | category | flops | bytes accessed | tf_op | source)
XLA Modules:
  0.0 165.8 jit_solution(3280089611787757365)
XLA Ops:
  4.8 7.4 %all-to-all-start.1 = ((s32[8,48,1]{1,2,0:T(1,128)}), s32[8,48,1]{1,2,0:T(1,128)S(1)}, u32[]{:S(2)}, u32[]{:S(2)}) async-start(s32[8,48,1]{1,2,0:T(1,128)} %bitcast.5), calls=%async_computation.1 | async-start | bytes 8192 | tf_op jit(solution)/shard_map/all_to_all | solution.py:96
  12.4 2.4 %scatter_custom_fusion.2 = bf16[384,512]{1,0:T(8,128)(2,1)} fusion(s32[192]{0:T(256)S(1)} %compare_select_fusion, bf16[192,512]{1,0:T(8,128)(2,1)} %param.6, f32[512]{0:T(512)S(1)} %mul.84, bf16[]{:T(256)} %constant.11.clone.1), kind=kCustom, calls=%fused_computation.141 | custom fusion | flops 294912 | bytes 591874 | tf_op jit(solution)/shard_map/scatter | solution.py:84
  14.8 3.8 %all-to-all-done.1 = s32[8,48,1]{1,2,0:T(1,128)S(1)} async-done(((s32[8,48,1]{1,2,0:T(1,128)}), s32[8,48,1]{1,2,0:T(1,128)S(1)}, u32[]{:S(2)}, u32[]{:S(2)}) %all-to-all-start.1) | async-done | bytes 1568 | tf_op jit(solution)/shard_map/all_to_all | solution.py:96
  18.6 3.5 %all-to-all-start.2 = ((bf16[8,48,512]{2,1,0:T(8,128)(2,1)}), bf16[8,48,512]{2,1,0:T(8,128)(2,1)S(1)}, u32[]{:S(2)}, u32[]{:S(2)}) async-start(bf16[8,48,512]{2,1,0:T(8,128)(2,1)} %bitcast.6), calls=%async_computation.2 | async-start | bytes 786432 | tf_op jit(solution)/shard_map/all_to_all | solution.py:92
  22.1 2.4 %scatter_custom_fusion = bf16[384,512]{1,0:T(8,128)(2,1)} fusion(s32[192]{0:T(256)S(1)} %compare_select_fusion, bf16[192,512]{1,0:T(8,128)(2,1)} %param.7, bf16[]{:T(256)} %constant.11.clone.1), kind=kCustom, calls=%fused_computation.148 | custom fusion | bytes 393728 | tf_op jit(solution)/shard_map/scatter | solution.py:84
  24.5 8.0 %all-to-all-done.2 = bf16[8,48,512]{2,1,0:T(8,128)(2,1)S(1)} async-done(((bf16[8,48,512]{2,1,0:T(8,128)(2,1)}), bf16[8,48,512]{2,1,0:T(8,128)(2,1)S(1)}, u32[]{:S(2)}, u32[]{:S(2)}) %all-to-all-start.2) | async-done | bytes 393248 | tf_op jit(solution)/shard_map/all_to_all | solution.py:92
  32.5 3.7 %all-to-all-start = ((bf16[8,48,512]{2,1,0:T(8,128)(2,1)}), bf16[8,48,512]{2,1,0:T(8,128)(2,1)S(1)}, u32[]{:S(2)}, u32[]{:S(2)}) async-start(bf16[8,48,512]{2,1,0:T(8,128)(2,1)} %bitcast.3), calls=%async_computation | async-start | bytes 786432 | tf_op jit(solution)/shard_map/all_to_all | solution.py:93
  36.2 2.4 %scatter_custom_fusion.3 = bf16[384,512]{1,0:T(8,128)(2,1)} fusion(s32[192]{0:T(256)S(1)} %compare_select_fusion, bf16[192,512]{1,0:T(8,128)(2,1)} %param.9, bf16[]{:T(256)} %constant.11.clone.1), kind=kCustom, calls=%fused_computation.145 | custom fusion | bytes 393728 | tf_op jit(solution)/shard_map/scatter | solution.py:84
  38.6 8.6 %all-to-all-done = bf16[8,48,512]{2,1,0:T(8,128)(2,1)S(1)} async-done(((bf16[8,48,512]{2,1,0:T(8,128)(2,1)}), bf16[8,48,512]{2,1,0:T(8,128)(2,1)S(1)}, u32[]{:S(2)}, u32[]{:S(2)}) %all-to-all-start) | async-done | bytes 393248 | tf_op jit(solution)/shard_map/all_to_all | solution.py:93
  47.2 3.7 %all-to-all-start.3 = ((bf16[8,48,512]{2,1,0:T(8,128)(2,1)}), bf16[8,48,512]{2,1,0:T(8,128)(2,1)S(1)}, u32[]{:S(2)}, u32[]{:S(2)}) async-start(bf16[8,48,512]{2,1,0:T(8,128)(2,1)} %bitcast.8), calls=%async_computation.3 | async-start | bytes 786432 | tf_op jit(solution)/shard_map/all_to_all | solution.py:95
  50.9 2.4 %scatter_custom_fusion.4 = bf16[384,512]{1,0:T(8,128)(2,1)} fusion(s32[192]{0:T(256)S(1)} %compare_select_fusion, bf16[192,512]{1,0:T(8,128)(2,1)} %param.8, bf16[]{:T(256)} %constant.11.clone.1), kind=kCustom, calls=%fused_computation.143 | custom fusion | bytes 393728 | tf_op jit(solution)/shard_map/scatter | solution.py:84
  55.9 6.5 %all-to-all-done.3 = bf16[8,48,512]{2,1,0:T(8,128)(2,1)S(1)} async-done(((bf16[8,48,512]{2,1,0:T(8,128)(2,1)}), bf16[8,48,512]{2,1,0:T(8,128)(2,1)S(1)}, u32[]{:S(2)}, u32[]{:S(2)}) %all-to-all-start.3) | async-done | bytes 393248 | tf_op jit(solution)/shard_map/all_to_all | solution.py:95
  62.4 3.6 %all-to-all-start.4 = ((bf16[8,48,512]{2,1,0:T(8,128)(2,1)}), bf16[8,48,512]{2,1,0:T(8,128)(2,1)S(1)}, u32[]{:S(2)}, u32[]{:S(2)}) async-start(bf16[8,48,512]{2,1,0:T(8,128)(2,1)} %bitcast.10), calls=%async_computation.4 | async-start | bytes 786432 | tf_op jit(solution)/shard_map/all_to_all | solution.py:94
  66.0 2.3 %fusion.167 = (bf16[384,1,64]{2,1,0:T(2,128)(2,1)S(1)}, bf16[384,1,64]{2,1,0:T(2,128)(2,1)S(1)}, bf16[384,1,64]{2,1,0:T(2,128)(2,1)}, bf16[384,1,64]{2,1,0:T(2,1...) fusion(bf16[384,4,128]{2,1,0:T(4,128)(2,1)S(1)} %reshape.660), kind=kLoop, calls=%fused_computation.266 | loop fusion | bytes 786432 | tf_op jit(solution)/shard_map/slice | solution.py:49
  68.3 1.7 %copy.113 = bf16[384,1,64]{0,2,1:T(8,128)(2,1)} copy(bf16[384,1,64]{2,1,0:T(2,128)(2,1)} %get-tuple-element.29) | data formatting | bytes 98304 | tf_op jit(solution)/shard_map/slice | solution.py:49
  73.6 2.3 %fusion.166 = (bf16[384,1,64]{2,1,0:T(2,128)(2,1)S(1)}, bf16[384,1,64]{2,1,0:T(2,128)(2,1)}, bf16[384,1,64]{2,1,0:T(2,128)(2,1)}, bf16[384,1,64]{2,1,0:T(2,128)(...) fusion(bf16[384,4,128]{2,1,0:T(4,128)(2,1)S(1)} %reshape.664), kind=kLoop, calls=%fused_computation.265 | loop fusion | bytes 786432 | tf_op jit(solution)/shard_map/slice | solution.py:51
  77.6 2.4 %fusion.165 = (bf16[384,1,64]{2,1,0:T(2,128)(2,1)}, bf16[384,1,64]{2,1,0:T(2,128)(2,1)}, bf16[384,1,64]{2,1,0:T(2,128)(2,1)}, bf16[384,1,64]{2,1,0:T(2,128)(2,1)...) fusion(bf16[384,4,128]{2,1,0:T(4,128)(2,1)S(1)} %reshape.666), kind=kLoop, calls=%fused_computation.264 | loop fusion | bytes 786432 | tf_op jit(solution)/shard_map/slice | solution.py:50
  93.5 1.7 %fusion.51 = bf16[384,64]{0,1:T(8,128)(2,1)} fusion(f32[384,384]{0,1:T(8,128)S(1)} %get-tuple-element.46, bf16[384,1,64]{0,2,1:T(8,128)(2,1)} %copy.137), kind=kOutput, calls=%fused_computation.115 | convolution fusion | flops 19046400 | bytes 688128 | tf_op jit(solution)/shard_map/hij,ihe->jhe/dot_general | solution.py:25
  115.3 5.2 %all-to-all-start.7 = ((bf16[8,48,512]{2,1,0:T(8,128)(2,1)}), bf16[8,48,512]{2,1,0:T(8,128)(2,1)S(1)}, u32[]{:S(2)}, u32[]{:S(2)}) async-start(bf16[8,48,512]{2,1,0:T(8,128)(2,1)} %all_to_all.70), calls=%async_computation.7 | async-start | bytes 786432 | tf_op jit(solution)/shard_map/all_to_all | solution.py:112
  133.2 6.0 %all-to-all-start.6 = ((bf16[8,48,512]{2,1,0:T(8,128)(2,1)}), bf16[8,48,512]{2,1,0:T(8,128)(2,1)S(1)}, u32[]{:S(2)}, u32[]{:S(2)}) async-start(bf16[8,48,512]{2,1,0:T(8,128)(2,1)} %all_to_all.67), calls=%async_computation.6 | async-start | bytes 786432 | tf_op jit(solution)/shard_map/all_to_all | solution.py:109
  141.4 8.1 %all-to-all-done.6 = bf16[8,48,512]{2,1,0:T(8,128)(2,1)S(1)} async-done(((bf16[8,48,512]{2,1,0:T(8,128)(2,1)}), bf16[8,48,512]{2,1,0:T(8,128)(2,1)S(1)}, u32[]{:S(2)}, u32[]{:S(2)}) %all-to-all-start.6) | async-done | bytes 393248 | tf_op jit(solution)/shard_map/all_to_all | solution.py:109
  149.5 3.7 %all-to-all-start.5 = ((bf16[8,48,512]{2,1,0:T(8,128)(2,1)}), bf16[8,48,512]{2,1,0:T(8,128)(2,1)S(1)}, u32[]{:S(2)}, u32[]{:S(2)}) async-start(bf16[8,48,512]{2,1,0:T(8,128)(2,1)} %all_to_all.64), calls=%async_computation.5 | async-start | bytes 786432 | tf_op jit(solution)/shard_map/all_to_all | solution.py:106
  153.2 1.7 %gather_fusion.2 = bf16[192,512]{1,0:T(8,128)(2,1)} fusion(bf16[384,512]{1,0:T(8,128)(2,1)S(1)} %bitcast.454, s32[1024]{0:T(1024)S(1)} %pad_clamp_fusion), kind=kCustom, calls=%fused_computation.2 | custom fusion | bytes 393984 | tf_op jit(solution)/shard_map/gather | solution.py:117
  156.6 7.5 %all-to-all-done.5 = bf16[8,48,512]{2,1,0:T(8,128)(2,1)S(1)} async-done(((bf16[8,48,512]{2,1,0:T(8,128)(2,1)}), bf16[8,48,512]{2,1,0:T(8,128)(2,1)S(1)}, u32[]{:S(2)}, u32[]{:S(2)}) %all-to-all-start.5) | async-done | bytes 393248 | tf_op jit(solution)/shard_map/all_to_all | solution.py:106
  (275 shorter events, 63.4 us)
Async XLA Ops:
  2.9 48.0 %copy-start.72 = (s32[192]{0:T(256)}, s32[192]{0:T(256)S(1)}, u32[]{:S(2)}) copy-start(s32[192]{0:T(256)S(1)} %compare_select_fusion) | copy-start | bytes 2308
  4.8 7.4 %copy-start.74 = (f32[8]{0:T(128)S(1)}, f32[8]{0:T(128)}, u32[]{:S(2)}) copy-start(f32[8]{0:T(128)} %param.11) | copy-start | bytes 100
  4.8 13.8 %all-to-all-start.1 = ((s32[8,48,1]{1,2,0:T(1,128)}), s32[8,48,1]{1,2,0:T(1,128)S(1)}, u32[]{:S(2)}, u32[]{:S(2)}) async-start(s32[8,48,1]{1,2,0:T(1,128)} %bitcast.5), calls=%async_computation.1 | async-start | bytes 8192 | tf_op jit(solution)/shard_map/all_to_all | solution.py:96
  18.6 13.9 %all-to-all-start.2 = ((bf16[8,48,512]{2,1,0:T(8,128)(2,1)}), bf16[8,48,512]{2,1,0:T(8,128)(2,1)S(1)}, u32[]{:S(2)}, u32[]{:S(2)}) async-start(bf16[8,48,512]{2,1,0:T(8,128)(2,1)} %bitcast.6), calls=%async_computation.2 | async-start | bytes 786432 | tf_op jit(solution)/shard_map/all_to_all | solution.py:92
  32.5 14.7 %all-to-all-start = ((bf16[8,48,512]{2,1,0:T(8,128)(2,1)}), bf16[8,48,512]{2,1,0:T(8,128)(2,1)S(1)}, u32[]{:S(2)}, u32[]{:S(2)}) async-start(bf16[8,48,512]{2,1,0:T(8,128)(2,1)} %bitcast.3), calls=%async_computation | async-start | bytes 786432 | tf_op jit(solution)/shard_map/all_to_all | solution.py:93
  47.2 15.2 %all-to-all-start.3 = ((bf16[8,48,512]{2,1,0:T(8,128)(2,1)}), bf16[8,48,512]{2,1,0:T(8,128)(2,1)S(1)}, u32[]{:S(2)}, u32[]{:S(2)}) async-start(bf16[8,48,512]{2,1,0:T(8,128)(2,1)} %bitcast.8), calls=%async_computation.3 | async-start | bytes 786432 | tf_op jit(solution)/shard_map/all_to_all | solution.py:95
  62.4 15.1 %all-to-all-start.4 = ((bf16[8,48,512]{2,1,0:T(8,128)(2,1)}), bf16[8,48,512]{2,1,0:T(8,128)(2,1)S(1)}, u32[]{:S(2)}, u32[]{:S(2)}) async-start(bf16[8,48,512]{2,1,0:T(8,128)(2,1)} %bitcast.10), calls=%async_computation.4 | async-start | bytes 786432 | tf_op jit(solution)/shard_map/all_to_all | solution.py:94
  72.3 9.7 %copy-start.24 = (bf16[384,1,64]{0,2,1:T(8,128)(2,1)}, bf16[384,1,64]{0,2,1:T(8,128)(2,1)S(1)}, u32[]{:S(2)}) copy-start(bf16[384,1,64]{0,2,1:T(8,128)(2,1)S(1)} %copy.103) | copy-start | bytes 147460
  72.4 10.4 %copy-start.42 = (bf16[384,1,64]{0,2,1:T(8,128)(2,1)}, bf16[384,1,64]{0,2,1:T(8,128)(2,1)S(1)}, u32[]{:S(2)}) copy-start(bf16[384,1,64]{0,2,1:T(8,128)(2,1)S(1)} %copy.99) | copy-start | bytes 147460
  72.5 10.3 %copy-start.44 = (bf16[384,1,64]{0,2,1:T(8,128)(2,1)}, bf16[384,1,64]{0,2,1:T(8,128)(2,1)S(1)}, u32[]{:S(2)}) copy-start(bf16[384,1,64]{0,2,1:T(8,128)(2,1)S(1)} %copy.98) | copy-start | bytes 147460
  72.6 10.5 %copy-start.50 = (bf16[384,1,64]{0,2,1:T(8,128)(2,1)}, bf16[384,1,64]{0,2,1:T(8,128)(2,1)S(1)}, u32[]{:S(2)}) copy-start(bf16[384,1,64]{0,2,1:T(8,128)(2,1)S(1)} %copy.94) | copy-start | bytes 147460
  72.8 10.4 %copy-start.52 = (bf16[384,1,64]{0,2,1:T(8,128)(2,1)}, bf16[384,1,64]{0,2,1:T(8,128)(2,1)S(1)}, u32[]{:S(2)}) copy-start(bf16[384,1,64]{0,2,1:T(8,128)(2,1)S(1)} %copy.93) | copy-start | bytes 147460
  72.9 10.6 %copy-start.38 = (bf16[384,1,64]{0,2,1:T(8,128)(2,1)}, bf16[384,1,64]{0,2,1:T(8,128)(2,1)S(1)}, u32[]{:S(2)}) copy-start(bf16[384,1,64]{0,2,1:T(8,128)(2,1)S(1)} %copy.89) | copy-start | bytes 147460
  73.0 10.5 %copy-start.40 = (bf16[384,1,64]{0,2,1:T(8,128)(2,1)}, bf16[384,1,64]{0,2,1:T(8,128)(2,1)S(1)}, u32[]{:S(2)}) copy-start(bf16[384,1,64]{0,2,1:T(8,128)(2,1)S(1)} %copy.88) | copy-start | bytes 147460
  73.1 10.7 %copy-start.36 = (bf16[384,1,64]{0,2,1:T(8,128)(2,1)}, bf16[384,1,64]{0,2,1:T(8,128)(2,1)S(1)}, u32[]{:S(2)}) copy-start(bf16[384,1,64]{0,2,1:T(8,128)(2,1)S(1)} %copy.119) | copy-start | bytes 147460
  73.2 10.6 %copy-start.28 = (bf16[384,1,64]{0,2,1:T(8,128)(2,1)}, bf16[384,1,64]{0,2,1:T(8,128)(2,1)S(1)}, u32[]{:S(2)}) copy-start(bf16[384,1,64]{0,2,1:T(8,128)(2,1)S(1)} %copy.118) | copy-start | bytes 147460
  73.4 10.7 %copy-start.46 = (bf16[384,1,64]{0,2,1:T(8,128)(2,1)}, bf16[384,1,64]{0,2,1:T(8,128)(2,1)S(1)}, u32[]{:S(2)}) copy-start(bf16[384,1,64]{0,2,1:T(8,128)(2,1)S(1)} %copy.84) | copy-start | bytes 147460
  73.5 10.6 %copy-start.48 = (bf16[384,1,64]{0,2,1:T(8,128)(2,1)}, bf16[384,1,64]{0,2,1:T(8,128)(2,1)S(1)}, u32[]{:S(2)}) copy-start(bf16[384,1,64]{0,2,1:T(8,128)(2,1)S(1)} %copy.82) | copy-start | bytes 147460
  115.3 5.2 %copy-start.5 = (bf16[384,1,64]{2,1,0:T(2,128)(2,1)S(1)}, bf16[384,1,64]{2,1,0:T(2,128)(2,1)}, u32[]{:S(2)}) copy-start(bf16[384,1,64]{2,1,0:T(2,128)(2,1)} %get-tuple-element.13) | copy-start | bytes 147460
  115.3 17.9 %all-to-all-start.7 = ((bf16[8,48,512]{2,1,0:T(8,128)(2,1)}), bf16[8,48,512]{2,1,0:T(8,128)(2,1)S(1)}, u32[]{:S(2)}, u32[]{:S(2)}) async-start(bf16[8,48,512]{2,1,0:T(8,128)(2,1)} %all_to_all.70), calls=%async_computation.7 | async-start | bytes 786432 | tf_op jit(solution)/shard_map/all_to_all | solution.py:112
  133.2 6.0 %copy-start.25 = (bf16[384,1,64]{0,2,1:T(8,128)(2,1)S(1)}, bf16[384,1,64]{0,2,1:T(8,128)(2,1)}, u32[]{:S(2)}) copy-start(bf16[384,1,64]{0,2,1:T(8,128)(2,1)} %copy-done.24) | copy-start | bytes 147460
  133.2 16.4 %all-to-all-start.6 = ((bf16[8,48,512]{2,1,0:T(8,128)(2,1)}), bf16[8,48,512]{2,1,0:T(8,128)(2,1)S(1)}, u32[]{:S(2)}, u32[]{:S(2)}) async-start(bf16[8,48,512]{2,1,0:T(8,128)(2,1)} %all_to_all.67), calls=%async_computation.6 | async-start | bytes 786432 | tf_op jit(solution)/shard_map/all_to_all | solution.py:109
  141.4 11.8 %copy-start.73 = (s32[192]{0:T(256)S(1)}, s32[192]{0:T(256)}, u32[]{:S(2)}) copy-start(s32[192]{0:T(256)} %copy-done.72) | copy-start | bytes 2308
  149.5 14.5 %all-to-all-start.5 = ((bf16[8,48,512]{2,1,0:T(8,128)(2,1)}), bf16[8,48,512]{2,1,0:T(8,128)(2,1)S(1)}, u32[]{:S(2)}, u32[]{:S(2)}) async-start(bf16[8,48,512]{2,1,0:T(8,128)(2,1)} %all_to_all.64), calls=%async_computation.5 | async-start | bytes 786432 | tf_op jit(solution)/shard_map/all_to_all | solution.py:106
  (59 other events, 65.3 us)
where the time goes:
time: 168 us; the launch traced here: 166 us
  local copies, waits for them, and re-layouts  55.4 us (33%)
  waiting for transfers between devices  43.4 us (26%)
  starting transfers between devices  36.7 us (22%)
  matrix products  20.4 us (12%)
  other arithmetic  8.4 us (5%)
    unnamed x158, local copies, waits for them, and re-layouts  20.3 us
    all_to_all x1, waiting for transfers between devices, local(): lax.all_to_all(sent_key, 'tile', split_axis=0, concat_axis=0, tiled=True)  8.59 us
    scatter x4, local copies, waits for them, and re-layouts, spread(): jnp.zeros((capacity,) + source.shape[1:], source.dtype).at[slot_index]  8.47 us
    all_to_all x1, waiting for transfers between devices, local(): lax.all_to_all(grad_key.reshape(capacity, columns), 'tile', split_axis=0,...  8.09 us
    all_to_all x1, waiting for transfers between devices, local(): lax.all_to_all(sent_query, 'tile', split_axis=0, concat_axis=0, tiled=True)  8.02 us
    all_to_all x1, waiting for transfers between devices, local(): lax.all_to_all(grad_raw.reshape(capacity, columns), 'tile', split_axis=0,...  7.47 us
    all_to_all x1, starting transfers between devices, local(): lax.all_to_all(flags, 'tile', split_axis=0, concat_axis=0, tiled=True)  7.41 us
    all_to_all x1, waiting for transfers between devices, local(): lax.all_to_all(sent_dout, 'tile', split_axis=0, concat_axis=0, tiled=True)  6.49 us
  transfers between devices with their start and end apart: 8, of which 7 were waited for; matrix products, arithmetic and copies ran while one was open for 19% of the time, Pallas kernels for 0%

commit v1 on v0

--- a/solution.py
+++ b/solution.py
@@ -1,9 +1,279 @@
+import functools
 import math
 
 import jax
 import jax.numpy as jnp
 from jax import lax
+from jax.experimental import pallas as pl
+from jax.experimental.pallas import tpu as pltpu
 from jax.sharding import PartitionSpec as P
+
+MESH = pl.DeviceIdType.MESH
+CONTRACT_LANES = (((1,), (1,)), ((), ()))
+
+
+def dot(left, right):
+    return jnp.dot(left, right, preferred_element_type=jnp.float32)
+
+
+def swap_halves(tile):
+    return pltpu.roll(tile, tile.shape[1] // 2, 1)
+
+
+def exchange_kernel(
+    n,
+    slot,
+    head_size,
+    ids_ref,
+    scale_ref,
+    q_ref,
+    k_ref,
+    v_ref,
+    g_ref,
+    oq_ref,
+    ok_ref,
+    ov_ref,
+    send_place,
+    send_qk,
+    send_vg,
+    got_place,
+    got_qk,
+    got_vg,
+    region_qk,
+    region_vg,
+    bias,
+    probs,
+    probs_low,
+    dscores,
+    out_kv,
+    out_q,
+    ret_kv,
+    ret_q,
+    back_kv,
+    back_q,
+    send_sem,
+    recv_sem,
+):
+    me = lax.axis_index("tile")
+    tokens = q_ref.shape[0]
+    capacity = n * slot
+    width = 2 * head_size
+    half = tokens // 2
+    f32, bf16 = jnp.float32, jnp.bfloat16
+    root = 1.0 / math.sqrt(head_size)
+
+    barrier = pltpu.get_barrier_semaphore()
+    for d in range(1, n):
+        pl.semaphore_signal(
+            barrier, inc=1, device_id={"tile": lax.rem(me + d, n)}, device_id_type=MESH
+        )
+
+    def low_lanes(rows):
+        return lax.broadcasted_iota(jnp.int32, (rows, width), 1) < head_size
+
+    low = low_lanes(tokens)
+    for pair in range(n // 2):
+        cols = slice(pair * width, (pair + 1) * width)
+        lane_scale = jnp.where(low, scale_ref[2 * pair] * root, scale_ref[2 * pair + 1] * root)
+        q = (q_ref[:, cols].astype(f32) * lane_scale).astype(bf16).astype(f32)
+        k = k_ref[:, cols].astype(f32)
+        v = v_ref[:, cols].astype(f32)
+        g = g_ref[:, cols].astype(f32)
+        send_qk[2 * pair] = jnp.where(low, q, swap_halves(k)).astype(bf16)
+        send_qk[2 * pair + 1] = jnp.where(low, swap_halves(q), k).astype(bf16)
+        send_vg[2 * pair] = jnp.where(low, v, swap_halves(g)).astype(bf16)
+        send_vg[2 * pair + 1] = jnp.where(low, swap_halves(v), g).astype(bf16)
+
+    ids = ids_ref[...]
+    mine = (lax.broadcasted_iota(jnp.int32, (n, tokens), 0) == ids).astype(f32)
+    earlier = (
+        lax.broadcasted_iota(jnp.int32, (tokens, tokens), 0)
+        < lax.broadcasted_iota(jnp.int32, (tokens, tokens), 1)
+    ).astype(bf16)
+    rank = jnp.sum(dot(mine.astype(bf16), earlier) * mine, axis=0, keepdims=True)
+    send_place[...] = jnp.broadcast_to(ids.astype(f32) * slot + rank, (8, tokens))
+
+    pl.semaphore_wait(barrier, n - 1)
+
+    def remote(kind, d, src, dst, peer):
+        copy = pltpu.make_async_remote_copy(
+            src_ref=src,
+            dst_ref=dst,
+            send_sem=send_sem.at[kind, d],
+            recv_sem=recv_sem.at[kind, d],
+            device_id={"tile": peer},
+            device_id_type=MESH,
+        )
+        copy.start()
+        return copy
+
+    order = sorted(range(1, n), key=lambda d: -min(d, n - d))
+    place_copies, qk_copies, vg_copies = {}, {}, {}
+    for d in order:
+        peer = lax.rem(me + d, n)
+        place_copies[d] = remote(0, d, send_place, got_place.at[d], peer)
+        qk_copies[d] = remote(1, d, send_qk.at[peer], got_qk.at[d], peer)
+    for d in order:
+        peer = lax.rem(me + d, n)
+        vg_copies[d] = remote(2, d, send_vg.at[peer], got_vg.at[d], peer)
+
+    got_place[0] = send_place[...]
+    arrivals = [0] + order[::-1]
+
+    def pick(d):
+        rows = lax.broadcasted_iota(jnp.int32, (capacity, tokens), 0).astype(f32)
+        return (rows == got_place[d][0:1, :]).astype(bf16)
+
+    for d in arrivals:
+        if d:
+            place_copies[d].wait_recv()
+            qk_copies[d].wait_recv()
+        block = got_qk[d] if d else send_qk[me]
+        region_qk[:, d] = dot(pick(d), block).astype(bf16).reshape(n, slot, width)
+
+    counts = jnp.zeros((n, capacity), f32)
+    table = jnp.zeros((8, tokens), f32)
+    slot_of = lax.broadcasted_iota(jnp.int32, (n, capacity), 1)
+    region_row = lax.broadcasted_iota(jnp.int32, (n, tokens), 0).astype(f32) * slot
+    for d in range(n):
+        place = got_place[d]
+        held = (place[0:1, :] >= region_row) & (place[0:1, :] < region_row + slot)
+        count = jnp.sum(held.astype(f32), axis=1, keepdims=True)
+        counts = jnp.where((slot_of >= d * slot) & (slot_of < (d + 1) * slot), count + d * slot, counts)
+        table = jnp.where(lax.broadcasted_iota(jnp.int32, (8, tokens), 0) == d, place, table)
+    bias_rows = jnp.where(slot_of.astype(f32) < counts, 0.0, -1e30)
+    bias_cols = jnp.transpose(bias_rows)
+    for r in range(n):
+        bias[r] = jnp.broadcast_to(bias_cols[:, r : r + 1], (capacity, 128))
+    place_cols = jnp.transpose(table)
+
+    low_cap = low_lanes(capacity)
+    blocks = [slice(b * 128, (b + 1) * 128) for b in range(capacity // 128)]
+
+    def score_step(r, carry):
+        qk = region_qk[r].reshape(capacity, width)
+        key_low = jnp.where(low_cap, swap_halves(qk.astype(f32)), 0.0).astype(bf16)
+        for b in blocks:
+            scores = lax.dot_general(
+                key_low, qk[b], CONTRACT_LANES, preferred_element_type=f32
+            ) + bias[r]
+            raw = jnp.exp(scores - jnp.max(scores, axis=0, keepdims=True))
+            probs[r, :, b] = raw * (1.0 / jnp.sum(raw, axis=0, keepdims=True))
+        return carry
+
+    lax.fori_loop(0, n, score_step, 0)
+
+    for d in arrivals:
+        if d:
+            vg_copies[d].wait_recv()
+        block = got_vg[d] if d else send_vg[me]
+        region_vg[:, d] = dot(pick(d), block).astype(bf16).reshape(n, slot, width)
+
+    my_scale = scale_ref[me] * root
+
+    def grad_step(r, carry):
+        qk = region_qk[r].reshape(capacity, width)
+        vg = region_vg[r].reshape(capacity, width)
+        vg_wide = vg.astype(f32)
+        value_low = jnp.where(low_cap, vg_wide, 0.0).astype(bf16)
+        gv = swap_halves(vg_wide).astype(bf16)
+        for b in blocks:
+            dprobs = lax.dot_general(
+                value_low, gv[b], CONTRACT_LANES, preferred_element_type=f32
+            )
+            weights = probs[r, :, b]
+            weights_low = weights.astype(bf16)
+            delta = jnp.sum(weights_low.astype(f32) * dprobs, axis=0, keepdims=True)
+            probs_low[:, b] = weights_low
+            dscores[:, b] = (weights * (dprobs - delta)).astype(bf16)
+        grads = jnp.where(low_cap, dot(dscores[...], qk), dot(probs_low[...], vg))
+        key_t = jnp.transpose(qk.astype(f32))[head_size:].astype(bf16)
+        raw_t = dot(key_t, dscores[...]).astype(bf16).astype(f32) * my_scale
+        raw = jnp.transpose(jnp.concatenate([raw_t, raw_t], axis=0))
+        out_kv[:, r] = grads.astype(bf16).reshape(n, slot, width)
+        out_q[:, r] = raw.astype(bf16).reshape(n, slot, width)
+        return carry
+
+    lax.fori_loop(0, n, grad_step, 0)
+
+    low_half = low_lanes(half)
+    back_copies = []
+    for d in order + [0]:
+        lanes = lax.broadcasted_iota(jnp.int32, (tokens, capacity), 1).astype(f32)
+        put = (lanes == place_cols[:, d : d + 1]).astype(bf16)
+        kv = dot(put, out_kv[d].reshape(capacity, width)).astype(bf16)
+        gq = dot(put, out_q[d].reshape(capacity, width))
+        gq = jnp.where(low_half, gq[:half], gq[half:]).astype(bf16)
+        if d:
+            peer = lax.rem(me + n - d, n)
+            ret_kv[d] = kv
+            ret_q[d] = gq
+            back_copies.append(remote(3, d, ret_kv.at[d], back_kv.at[me], peer))
+            back_copies.append(remote(4, d, ret_q.at[d], back_q.at[me], peer))
+        else:
+            back_kv[me] = kv
+            back_q[me] = gq
+    for copy in back_copies:
+        copy.wait_recv()
+
+    for pair in range(n // 2):
+        cols = slice(pair * width, (pair + 1) * width)
+        kv0, kv1 = back_kv[2 * pair].astype(f32), back_kv[2 * pair + 1].astype(f32)
+        gq0, gq1 = back_q[2 * pair].astype(f32), back_q[2 * pair + 1].astype(f32)
+        ok_ref[:, cols] = jnp.where(low, kv0, swap_halves(kv1)).astype(bf16)
+        ov_ref[:, cols] = jnp.where(low, swap_halves(kv0), kv1).astype(bf16)
+        oq_ref[:half, cols] = jnp.where(low_half, gq0, swap_halves(gq1)).astype(bf16)
+        oq_ref[half:, cols] = jnp.where(low_half, swap_halves(gq0), gq1).astype(bf16)
+
+    for copies in (place_copies, qk_copies, vg_copies):
+        for copy in copies.values():
+            copy.wait_send()
+    for copy in back_copies:
+        copy.wait_send()
+
+
+def by_heads(queries, key_rows, value_rows, grad_out, owner_shard, logit_scale):
+    n = lax.axis_size("tile")
+    tokens, columns = queries.shape
+    head_size = columns // n
+    capacity = 2 * tokens
+    slot = capacity // n
+    width = 2 * head_size
+    bf16, f32 = jnp.bfloat16, jnp.float32
+    vmem = pl.BlockSpec(memory_space=pltpu.VMEM)
+    smem = pl.BlockSpec(memory_space=pltpu.SMEM)
+    out = jax.ShapeDtypeStruct((tokens, columns), bf16)
+    return pl.pallas_call(
+        functools.partial(exchange_kernel, n, slot, head_size),
+        out_shape=(out, out, out),
+        in_specs=[vmem, smem, vmem, vmem, vmem, vmem],
+        out_specs=(vmem, vmem, vmem),
+        scratch_shapes=[
+            pltpu.VMEM((8, tokens), f32),
+            pltpu.VMEM((n, tokens, width), bf16),
+            pltpu.VMEM((n, tokens, width), bf16),
+            pltpu.VMEM((n, 8, tokens), f32),
+            pltpu.VMEM((n, tokens, width), bf16),
+            pltpu.VMEM((n, tokens, width), bf16),
+            pltpu.VMEM((n, n, slot, width), bf16),
+            pltpu.VMEM((n, n, slot, width), bf16),
+            pltpu.VMEM((n, capacity, 128), f32),
+            pltpu.VMEM((n, capacity, capacity), f32),
+            pltpu.VMEM((capacity, capacity), bf16),
+            pltpu.VMEM((capacity, capacity), bf16),
+            pltpu.VMEM((n, n, slot, width), bf16),
+            pltpu.VMEM((n, n, slot, width), bf16),
+            pltpu.VMEM((n, tokens, width), bf16),
+            pltpu.VMEM((n, tokens // 2, width), bf16),
+            pltpu.VMEM((n, tokens, width), bf16),
+            pltpu.VMEM((n, tokens // 2, width), bf16),
+            pltpu.SemaphoreType.DMA((5, n)),
+            pltpu.SemaphoreType.DMA((5, n)),
+        ],
+        compiler_params=pltpu.CompilerParams(
+            collective_id=0, has_side_effects=True, vmem_limit_bytes=56 * 1024 * 1024
+        ),
+    )(owner_shard.reshape(1, tokens), logit_scale, queries, key_rows, value_rows, grad_out)
 
 
 def attend_heads(query_heads, key_heads, value_heads, dout_heads, live_rows):
@@ -67,7 +337,7 @@
     return owner_shard * slot + rank
 
 
-def local(queries, key_rows, value_rows, grad_out, owner_shard, logit_scale):
+def by_regions(queries, key_rows, value_rows, grad_out, owner_shard, logit_scale):
     shards = lax.axis_size("tile")
     tok_rows, columns = queries.shape
     heads_here = logit_scale.shape[0]
@@ -117,6 +387,22 @@
     return (grad_queries, returned[1][slot_index], returned[2][slot_index])
 
 
+def local(queries, key_rows, value_rows, grad_out, owner_shard, logit_scale):
+    shards = lax.axis_size("tile")
+    tokens, columns = queries.shape
+    heads_here = logit_scale.shape[0]
+    slot = 2 * tokens // shards
+    fits = (
+        shards == heads_here == 8
+        and columns == heads_here * 64
+        and slot % 16 == 0
+        and (2 * tokens) % 128 == 0
+        and tokens % 32 == 0
+    )
+    plan = by_heads if fits else by_regions
+    return plan(queries, key_rows, value_rows, grad_out, owner_shard, logit_scale)
+
+
 def solution(mesh):
     return jax.shard_map(
         local,

time: 168 us -> 52.3 us (0.31); the launches traced: 166 us -> 52.1 us
  local copies, waits for them, and re-layouts: 55.4 us -> 3.33 us
  Pallas kernels: 0 us -> 48.2 us
  waiting for transfers between devices: 43.4 us -> 0 us
  starting transfers between devices: 36.7 us -> 0 us
  matrix products: 20.4 us -> 0 us
  other arithmetic: 8.4 us -> 0 us
    pallas_call x0 -> x1, Pallas kernels: none -> 48.2 us  [by_heads(): pl.pallas_call(functools.partial(exchange_kernel, n, slot, head_size), ou...]
    all_to_all x8 -> x0, waiting for transfers between devices: 43.4 us -> none  [the longest x1 8.59 us: local(): lax.all_to_all(sent_key, 'tile', split_axis=0, concat_axis=0, tiled=True)]
    all_to_all x8 -> x0, starting transfers between devices: 36.7 us -> none  [the longest x1 7.41 us: local(): lax.all_to_all(flags, 'tile', split_axis=0, concat_axis=0, tiled=True)]
    dot_general x48 -> x0, matrix products: 20.4 us -> none  [the longest x8 5.18 us: attend_heads(): jnp.einsum('hij,ihe->jhe', weights_low, dout_heads, preferred_element_typ...]
    slice x29 -> x0, local copies, waits for them, and re-layouts: 17.5 us -> none  [the longest x9 5.42 us: attend_items(): value_items[:, item_index, lower:upper].reshape(capacity, 1, head_size)]
    unnamed x158 -> x7, local copies, waits for them, and re-layouts: 20.3 us -> 3.33 us
    scatter x4 -> x0, local copies, waits for them, and re-layouts: 8.47 us -> none  [spread(): jnp.zeros((capacity,) + source.shape[1:], source.dtype).at[slot_index]]
    gather x3 -> x0, local copies, waits for them, and re-layouts: 4.36 us -> none  [the longest x2 3.36 us: local(): return (grad_queries, returned[1][slot_index], returned[2][slot_index])]
  transfers between devices with their start and end apart: 8 -> 0, of which waited for: 7 -> 0; matrix products, arithmetic and copies ran while one was open for 19% -> 0% of each run, Pallas kernels for 0% -> 0%
where the time goes in v1:
time: 52.3 us; the launch traced here: 52.1 us
  Pallas kernels  48.2 us (92%)
  local copies, waits for them, and re-layouts  3.33 us (6%)
  between operations  0.65 us (1%)
    pallas_call x1, Pallas kernels, by_heads(): pl.pallas_call(functools.partial(exchange_kernel, n, slot, head_size), ou...  48.2 us
    unnamed x7, local copies, waits for them, and re-layouts  3.33 us

profile of v1, /device:TPU:0, one launch (start us, length us, event | category | flops | bytes accessed | tf_op | source)
XLA Modules:
  0.0 52.1 jit_solution(17812437692115390421)
XLA Ops:
  0.6 48.2 %shard_map.85 = (bf16[192,512]{1,0:T(8,128)(2,1)}, bf16[192,512]{1,0:T(8,128)(2,1)}, bf16[192,512]{1,0:T(8,128)(2,1)}) custom-call(s32[1,192]{1,0:T(1,128)} %bitcast.1, f32[8]{0:T(128)} %scale_ref.1, bf16[192,512]{1,0:T(8,128)(2,1)} %q_ref.1, bf16[192,512]{1,0:T(8,128)(2,1)} %k_ref.1, bf16[192,512]{1,0:T(8,128)(2,1)} %v_ref.1, bf16[192,512]{1,0:T(8,128)(2,1)} %g_ref.1), custom_call_target="tpu_custom_call" | custom-call | tf_op jit(solution)/shard_map/pallas_call | solution.py:246
  48.8 0.0 copy-start.1
  48.8 1.7 %copy.12 = bf16[192,512]{1,0:T(8,128)(2,1)} copy(bf16[192,512]{1,0:T(8,128)(2,1)} %get-tuple-element.6) | data formatting | bytes 393216
  50.5 0.0 copy-done.1
  50.5 0.0 copy-start
  50.5 0.7 %copy.13 = bf16[192,512]{1,0:T(8,128)(2,1)} copy(bf16[192,512]{1,0:T(8,128)(2,1)S(1)} %copy-done.1) | data formatting | bytes 393216
  51.1 0.3 copy-done
  51.5 0.7 %copy.14 = bf16[192,512]{1,0:T(8,128)(2,1)} copy(bf16[192,512]{1,0:T(8,128)(2,1)S(1)} %copy-done) | data formatting | bytes 393216
Async XLA Ops:
  48.8 1.7 %copy-start.1 = (bf16[192,512]{1,0:T(8,128)(2,1)S(1)}, bf16[192,512]{1,0:T(8,128)(2,1)}, u32[]{:S(2)}) copy-start(bf16[192,512]{1,0:T(8,128)(2,1)} %get-tuple-element.7) | copy-start | bytes 589828
  50.5 1.0 %copy-start = (bf16[192,512]{1,0:T(8,128)(2,1)S(1)}, bf16[192,512]{1,0:T(8,128)(2,1)}, u32[]{:S(2)}) copy-start(bf16[192,512]{1,0:T(8,128)(2,1)} %get-tuple-element.8) | copy-start | bytes 589828

commit v2 on v1

--- a/solution.py
+++ b/solution.py
@@ -26,31 +26,38 @@
     head_size,
     ids_ref,
     scale_ref,
+    q_hbm,
+    k_hbm,
+    v_hbm,
+    g_hbm,
+    back_kq,
+    back_v,
     q_ref,
     k_ref,
     v_ref,
     g_ref,
-    oq_ref,
-    ok_ref,
-    ov_ref,
     send_place,
     send_qk,
-    send_vg,
+    send_g,
+    send_v,
     got_place,
     got_qk,
-    got_vg,
+    got_g,
+    got_v,
     region_qk,
-    region_vg,
+    region_k,
+    region_kt,
+    region_g,
+    region_v,
     bias,
     probs,
     probs_low,
     dscores,
-    out_kv,
-    out_q,
-    ret_kv,
-    ret_q,
-    back_kv,
-    back_q,
+    out_v,
+    out_kq,
+    ret_v,
+    ret_kq,
+    load_sem,
     send_sem,
     recv_sem,
 ):
@@ -67,22 +74,17 @@
         pl.semaphore_signal(
             barrier, inc=1, device_id={"tile": lax.rem(me + d, n)}, device_id_type=MESH
         )
+    loads = [
+        pltpu.make_async_copy(src, dst, load_sem.at[i])
+        for i, (src, dst) in enumerate(
+            ((q_hbm, q_ref), (k_hbm, k_ref), (g_hbm, g_ref), (v_hbm, v_ref))
+        )
+    ]
+    for load in loads:
+        load.start()
 
     def low_lanes(rows):
         return lax.broadcasted_iota(jnp.int32, (rows, width), 1) < head_size
-
-    low = low_lanes(tokens)
-    for pair in range(n // 2):
-        cols = slice(pair * width, (pair + 1) * width)
-        lane_scale = jnp.where(low, scale_ref[2 * pair] * root, scale_ref[2 * pair + 1] * root)
-        q = (q_ref[:, cols].astype(f32) * lane_scale).astype(bf16).astype(f32)
-        k = k_ref[:, cols].astype(f32)
-        v = v_ref[:, cols].astype(f32)
-        g = g_ref[:, cols].astype(f32)
-        send_qk[2 * pair] = jnp.where(low, q, swap_halves(k)).astype(bf16)
-        send_qk[2 * pair + 1] = jnp.where(low, swap_halves(q), k).astype(bf16)
-        send_vg[2 * pair] = jnp.where(low, v, swap_halves(g)).astype(bf16)
-        send_vg[2 * pair + 1] = jnp.where(low, swap_halves(v), g).astype(bf16)
 
     ids = ids_ref[...]
     mine = (lax.broadcasted_iota(jnp.int32, (n, tokens), 0) == ids).astype(f32)
@@ -92,6 +94,20 @@
     ).astype(bf16)
     rank = jnp.sum(dot(mine.astype(bf16), earlier) * mine, axis=0, keepdims=True)
     send_place[...] = jnp.broadcast_to(ids.astype(f32) * slot + rank, (8, tokens))
+
+    low, low_half, low_cap = low_lanes(tokens), low_lanes(half), low_lanes(capacity)
+    pairs = [
+        (2 * pair, 2 * pair + 1, slice(pair * width, (pair + 1) * width))
+        for pair in range(n // 2)
+    ]
+    loads[0].wait()
+    loads[1].wait()
+    for one, two, cols in pairs:
+        lane_scale = jnp.where(low, scale_ref[one] * root, scale_ref[two] * root)
+        q = (q_ref[:, cols].astype(f32) * lane_scale).astype(bf16).astype(f32)
+        k = k_ref[:, cols].astype(f32)
+        send_qk[one] = jnp.where(low, q, swap_halves(k)).astype(bf16)
+        send_qk[two] = jnp.where(low, swap_halves(q), k).astype(bf16)
 
     pl.semaphore_wait(barrier, n - 1)
 
@@ -108,17 +124,29 @@
         return copy
 
     order = sorted(range(1, n), key=lambda d: -min(d, n - d))
-    place_copies, qk_copies, vg_copies = {}, {}, {}
+    arrivals = [0] + order[::-1]
+    place_copies, qk_copies, g_copies, v_copies = {}, {}, {}, {}
     for d in order:
         peer = lax.rem(me + d, n)
         place_copies[d] = remote(0, d, send_place, got_place.at[d], peer)
         qk_copies[d] = remote(1, d, send_qk.at[peer], got_qk.at[d], peer)
+
+    def fold(ref, send, load):
+        load.wait()
+        for one, two, cols in pairs:
+            top, bottom = ref[:half, cols].astype(f32), ref[half:, cols].astype(f32)
+            send[one] = jnp.where(low_half, top, swap_halves(bottom)).astype(bf16)
+            send[two] = jnp.where(low_half, swap_halves(top), bottom).astype(bf16)
+
+    fold(g_ref, send_g, loads[2])
+    fold(v_ref, send_v, loads[3])
+
     for d in order:
         peer = lax.rem(me + d, n)
-        vg_copies[d] = remote(2, d, send_vg.at[peer], got_vg.at[d], peer)
+        qk_copies[d].wait_send()
+        g_copies[d] = remote(2, d, send_g.at[peer], got_g.at[d], peer)
 
     got_place[0] = send_place[...]
-    arrivals = [0] + order[::-1]
 
     def pick(d):
         rows = lax.broadcasted_iota(jnp.int32, (capacity, tokens), 0).astype(f32)
@@ -129,7 +157,10 @@
             place_copies[d].wait_recv()
             qk_copies[d].wait_recv()
         block = got_qk[d] if d else send_qk[me]
-        region_qk[:, d] = dot(pick(d), block).astype(bf16).reshape(n, slot, width)
+        placed = dot(pick(d), block)
+        key_low = jnp.where(low_cap, swap_halves(placed), 0.0)
+        region_qk[:, d] = placed.astype(bf16).reshape(n, slot, width)
+        region_k[:, d] = key_low.astype(bf16).reshape(n, slot, width)
 
     counts = jnp.zeros((n, capacity), f32)
     table = jnp.zeros((8, tokens), f32)
@@ -139,97 +170,129 @@
         place = got_place[d]
         held = (place[0:1, :] >= region_row) & (place[0:1, :] < region_row + slot)
         count = jnp.sum(held.astype(f32), axis=1, keepdims=True)
-        counts = jnp.where((slot_of >= d * slot) & (slot_of < (d + 1) * slot), count + d * slot, counts)
+        here = (slot_of >= d * slot) & (slot_of < (d + 1) * slot)
+        counts = jnp.where(here, count + d * slot, counts)
         table = jnp.where(lax.broadcasted_iota(jnp.int32, (8, tokens), 0) == d, place, table)
-    bias_rows = jnp.where(slot_of.astype(f32) < counts, 0.0, -1e30)
-    bias_cols = jnp.transpose(bias_rows)
+    bias_cols = jnp.transpose(jnp.where(slot_of.astype(f32) < counts, 0.0, -1e30))
     for r in range(n):
         bias[r] = jnp.broadcast_to(bias_cols[:, r : r + 1], (capacity, 128))
     place_cols = jnp.transpose(table)
 
-    low_cap = low_lanes(capacity)
     blocks = [slice(b * 128, (b + 1) * 128) for b in range(capacity // 128)]
 
     def score_step(r, carry):
         qk = region_qk[r].reshape(capacity, width)
-        key_low = jnp.where(low_cap, swap_halves(qk.astype(f32)), 0.0).astype(bf16)
+        key_low = region_k[r].reshape(capacity, width)
         for b in blocks:
             scores = lax.dot_general(
                 key_low, qk[b], CONTRACT_LANES, preferred_element_type=f32
             ) + bias[r]
             raw = jnp.exp(scores - jnp.max(scores, axis=0, keepdims=True))
-            probs[r, :, b] = raw * (1.0 / jnp.sum(raw, axis=0, keepdims=True))
+            weights = raw * (1.0 / jnp.sum(raw, axis=0, keepdims=True))
+            probs[r, :, b] = weights
+            probs_low[r, :, b] = weights.astype(bf16)
+        region_kt[r] = jnp.transpose(qk.astype(f32))[head_size:].astype(bf16)
         return carry
 
-    lax.fori_loop(0, n, score_step, 0)
+    lax.fori_loop(0, n, score_step, 0, unroll=n // 2)
+
+    for d in order:
+        peer = lax.rem(me + d, n)
+        g_copies[d].wait_send()
+        v_copies[d] = remote(3, d, send_v.at[peer], got_v.at[d], peer)
+
+    def unfold(got, send, d):
+        folded = (got[d] if d else send[me]).astype(f32)
+        return jnp.concatenate([folded, swap_halves(folded)], axis=0).astype(bf16)
 
     for d in arrivals:
         if d:
-            vg_copies[d].wait_recv()
-        block = got_vg[d] if d else send_vg[me]
-        region_vg[:, d] = dot(pick(d), block).astype(bf16).reshape(n, slot, width)
+            g_copies[d].wait_recv()
+        placed = dot(pick(d), unfold(got_g, send_g, d))
+        region_g[:, d] = placed.astype(bf16).reshape(n, slot, width)
+
+    def value_step(r, carry):
+        grads = dot(probs_low[r], region_g[r].reshape(capacity, width))
+        out_v[:, r] = grads.astype(bf16).reshape(n, slot, width)
+        return carry
+
+    lax.fori_loop(0, n, value_step, 0, unroll=n // 2)
+
+    def put(d, source):
+        lanes = lax.broadcasted_iota(jnp.int32, (tokens, capacity), 1).astype(f32)
+        rows = (lanes == place_cols[:, d : d + 1]).astype(bf16)
+        return dot(rows, source[d].reshape(capacity, width))
+
+    back_copies = []
+    for d in order + [0]:
+        grads = put(d, out_v)
+        grads = jnp.where(low_half, grads[:half], swap_halves(grads[half:])).astype(bf16)
+        if d:
+            ret_v[d] = grads
+            peer = lax.rem(me + n - d, n)
+            back_copies.append(remote(4, d, ret_v.at[d], back_v.at[me], peer))
+        else:
+            back_v[me] = grads
+
+    for d in arrivals:
+        if d:
+            v_copies[d].wait_recv()
+        placed = jnp.where(low_cap, dot(pick(d), unfold(got_v, send_v, d)), 0.0)
+        region_v[:, d] = placed.astype(bf16).reshape(n, slot, width)
 
     my_scale = scale_ref[me] * root
 
     def grad_step(r, carry):
-        qk = region_qk[r].reshape(capacity, width)
-        vg = region_vg[r].reshape(capacity, width)
-        vg_wide = vg.astype(f32)
-        value_low = jnp.where(low_cap, vg_wide, 0.0).astype(bf16)
-        gv = swap_halves(vg_wide).astype(bf16)
+        value_low = region_v[r].reshape(capacity, width)
+        g = region_g[r].reshape(capacity, width)
         for b in blocks:
             dprobs = lax.dot_general(
-                value_low, gv[b], CONTRACT_LANES, preferred_element_type=f32
+                value_low, g[b], CONTRACT_LANES, preferred_element_type=f32
             )
-            weights = probs[r, :, b]
-            weights_low = weights.astype(bf16)
-            delta = jnp.sum(weights_low.astype(f32) * dprobs, axis=0, keepdims=True)
-            probs_low[:, b] = weights_low
-            dscores[:, b] = (weights * (dprobs - delta)).astype(bf16)
-        grads = jnp.where(low_cap, dot(dscores[...], qk), dot(probs_low[...], vg))
-        key_t = jnp.transpose(qk.astype(f32))[head_size:].astype(bf16)
-        raw_t = dot(key_t, dscores[...]).astype(bf16).astype(f32) * my_scale
+            delta = jnp.sum(
+                probs_low[r, :, b].astype(f32) * dprobs, axis=0, keepdims=True
+            )
+            dscores[r, :, b] = (probs[r, :, b] * (dprobs - delta)).astype(bf16)
+        grads = dot(dscores[r], region_qk[r].reshape(capacity, width))
+        raw_t = dot(region_kt[r], dscores[r]).astype(bf16).astype(f32) * my_scale
         raw = jnp.transpose(jnp.concatenate([raw_t, raw_t], axis=0))
-        out_kv[:, r] = grads.astype(bf16).reshape(n, slot, width)
-        out_q[:, r] = raw.astype(bf16).reshape(n, slot, width)
+        grads = jnp.where(low_cap, grads, raw)
+        out_kq[:, r] = grads.astype(bf16).reshape(n, slot, width)
         return carry
 
-    lax.fori_loop(0, n, grad_step, 0)
-
-    low_half = low_lanes(half)
-    back_copies = []
+    lax.fori_loop(0, n, grad_step, 0, unroll=n // 2)
+
     for d in order + [0]:
-        lanes = lax.broadcasted_iota(jnp.int32, (tokens, capacity), 1).astype(f32)
-        put = (lanes == place_cols[:, d : d + 1]).astype(bf16)
-        kv = dot(put, out_kv[d].reshape(capacity, width)).astype(bf16)
-        gq = dot(put, out_q[d].reshape(capacity, width))
-        gq = jnp.where(low_half, gq[:half], gq[half:]).astype(bf16)
+        grads = put(d, out_kq).astype(bf16)
         if d:
+            ret_kq[d] = grads
             peer = lax.rem(me + n - d, n)
-            ret_kv[d] = kv
-            ret_q[d] = gq
-            back_copies.append(remote(3, d, ret_kv.at[d], back_kv.at[me], peer))
-            back_copies.append(remote(4, d, ret_q.at[d], back_q.at[me], peer))
+            back_copies.append(remote(5, d, ret_kq.at[d], back_kq.at[me], peer))
         else:
-            back_kv[me] = kv
-            back_q[me] = gq
+            back_kq[me] = grads
     for copy in back_copies:
         copy.wait_recv()
-
-    for pair in range(n // 2):
-        cols = slice(pair * width, (pair + 1) * width)
-        kv0, kv1 = back_kv[2 * pair].astype(f32), back_kv[2 * pair + 1].astype(f32)
-        gq0, gq1 = back_q[2 * pair].astype(f32), back_q[2 * pair + 1].astype(f32)
-        ok_ref[:, cols] = jnp.where(low, kv0, swap_halves(kv1)).astype(bf16)
-        ov_ref[:, cols] = jnp.where(low, swap_halves(kv0), kv1).astype(bf16)
-        oq_ref[:half, cols] = jnp.where(low_half, gq0, swap_halves(gq1)).astype(bf16)
-        oq_ref[half:, cols] = jnp.where(low_half, swap_halves(gq0), gq1).astype(bf16)
-
-    for copies in (place_copies, qk_copies, vg_copies):
+    for copies in (place_copies, v_copies):
         for copy in copies.values():
             copy.wait_send()
     for copy in back_copies:
         copy.wait_send()
+
+
+def unpack_kernel(n, kq_ref, v_ref, oq_ref, ok_ref, ov_ref):
+    tokens, width = kq_ref.shape[1:]
+    half = tokens // 2
+    f32, bf16 = jnp.float32, jnp.bfloat16
+    low = lax.broadcasted_iota(jnp.int32, (tokens, width), 1) < width // 2
+    low_half = lax.broadcasted_iota(jnp.int32, (half, width), 1) < width // 2
+    for pair in range(n // 2):
+        cols = slice(pair * width, (pair + 1) * width)
+        kq0, kq1 = kq_ref[2 * pair].astype(f32), kq_ref[2 * pair + 1].astype(f32)
+        v0, v1 = v_ref[2 * pair].astype(f32), v_ref[2 * pair + 1].astype(f32)
+        ok_ref[:, cols] = jnp.where(low, kq0, swap_halves(kq1)).astype(bf16)
+        oq_ref[:, cols] = jnp.where(low, swap_halves(kq0), kq1).astype(bf16)
+        ov_ref[:half, cols] = jnp.where(low_half, v0, swap_halves(v1)).astype(bf16)
+        ov_ref[half:, cols] = jnp.where(low_half, swap_halves(v0), v1).astype(bf16)
 
 
 def by_heads(queries, key_rows, value_rows, grad_out, owner_shard, logit_scale):
@@ -242,38 +305,41 @@
     bf16, f32 = jnp.bfloat16, jnp.float32
     vmem = pl.BlockSpec(memory_space=pltpu.VMEM)
     smem = pl.BlockSpec(memory_space=pltpu.SMEM)
+    anywhere = pl.BlockSpec(memory_space=pltpu.HBM)
+    full = pltpu.VMEM((n, tokens, width), bf16)
+    folded = pltpu.VMEM((n, tokens // 2, width), bf16)
+    region = pltpu.VMEM((n, n, slot, width), bf16)
+    square = (n, capacity, capacity)
+    grant = 67043328 - 3 * n * tokens * width - 64 * 1024
+    back_kq, back_v = pl.pallas_call(
+        functools.partial(exchange_kernel, n, slot, head_size),
+        out_shape=(
+            pltpu.VMEM((n, tokens, width), bf16),
+            pltpu.VMEM((n, tokens // 2, width), bf16),
+        ),
+        in_specs=[vmem, smem, anywhere, anywhere, anywhere, anywhere],
+        out_specs=(vmem, vmem),
+        scratch_shapes=[pltpu.VMEM((tokens, columns), bf16)] * 4
+        + [pltpu.VMEM((8, tokens), f32), full, folded, folded]
+        + [pltpu.VMEM((n, 8, tokens), f32), full, folded, folded]
+        + [region, region, pltpu.VMEM((n, head_size, capacity), bf16), region, region]
+        + [pltpu.VMEM((n, capacity, 128), f32), pltpu.VMEM(square, f32)]
+        + [pltpu.VMEM(square, bf16), pltpu.VMEM(square, bf16)]
+        + [region, region, folded, full]
+        + [pltpu.SemaphoreType.DMA((4,))]
+        + [pltpu.SemaphoreType.DMA((6, n))] * 2,
+        compiler_params=pltpu.CompilerParams(
+            collective_id=0, has_side_effects=True, vmem_limit_bytes=grant
+        ),
+    )(owner_shard.reshape(1, tokens), logit_scale, queries, key_rows, value_rows, grad_out)
     out = jax.ShapeDtypeStruct((tokens, columns), bf16)
     return pl.pallas_call(
-        functools.partial(exchange_kernel, n, slot, head_size),
+        functools.partial(unpack_kernel, n),
         out_shape=(out, out, out),
-        in_specs=[vmem, smem, vmem, vmem, vmem, vmem],
+        in_specs=[vmem, vmem],
         out_specs=(vmem, vmem, vmem),
-        scratch_shapes=[
-            pltpu.VMEM((8, tokens), f32),
-            pltpu.VMEM((n, tokens, width), bf16),
-            pltpu.VMEM((n, tokens, width), bf16),
-            pltpu.VMEM((n, 8, tokens), f32),
-            pltpu.VMEM((n, tokens, width), bf16),
-            pltpu.VMEM((n, tokens, width), bf16),
-            pltpu.VMEM((n, n, slot, width), bf16),
-            pltpu.VMEM((n, n, slot, width), bf16),
-            pltpu.VMEM((n, capacity, 128), f32),
-            pltpu.VMEM((n, capacity, capacity), f32),
-            pltpu.VMEM((capacity, capacity), bf16),
-            pltpu.VMEM((capacity, capacity), bf16),
-            pltpu.VMEM((n, n, slot, width), bf16),
-            pltpu.VMEM((n, n, slot, width), bf16),
-            pltpu.VMEM((n, tokens, width), bf16),
-            pltpu.VMEM((n, tokens // 2, width), bf16),
-            pltpu.VMEM((n, tokens, width), bf16),
-            pltpu.VMEM((n, tokens // 2, width), bf16),
-            pltpu.SemaphoreType.DMA((5, n)),
-            pltpu.SemaphoreType.DMA((5, n)),
-        ],
-        compiler_params=pltpu.CompilerParams(
-            collective_id=0, has_side_effects=True, vmem_limit_bytes=56 * 1024 * 1024
-        ),
-    )(owner_shard.reshape(1, tokens), logit_scale, queries, key_rows, value_rows, grad_out)
+        compiler_params=pltpu.CompilerParams(vmem_limit_bytes=8 * 1024 * 1024),
+    )(back_kq, back_v)
 
 
 def attend_heads(query_heads, key_heads, value_heads, dout_heads, live_rows):

time: 52.3 us -> 47.7 us (0.912)
  local copies, waits for them, and re-layouts: 3.33 us -> 0 us
  Pallas kernels: 48.2 us -> 46.9 us
    unnamed x7 -> x0, local copies, waits for them, and re-layouts: 3.33 us -> none
    pallas_call x1, Pallas kernels: 48.2 us -> 45.9 us  [by_heads(): pl.pallas_call(functools.partial(exchange_kernel, n, slot, head_size), ou...]
    pallas_call x0 -> x1, Pallas kernels: none -> 1.04 us  [by_heads(): pl.pallas_call(functools.partial(unpack_kernel, n), out_shape=(out, out,...]
where the time goes in v2:
time: 47.7 us; the launch traced here: 47.5 us
  Pallas kernels  46.9 us (98%)
  between operations  0.64 us (1%)
    pallas_call x1, Pallas kernels, by_heads(): pl.pallas_call(functools.partial(exchange_kernel, n, slot, head_size), ou...  45.9 us
    pallas_call x1, Pallas kernels, by_heads(): pl.pallas_call(functools.partial(unpack_kernel, n), out_shape=(out, out,...  1.04 us

profile of v2, /device:TPU:0, one launch (start us, length us, event | category | flops | bytes accessed | tf_op | source)
XLA Modules:
  0.0 47.5 jit_solution(15945220511725957442)
XLA Ops:
  0.6 45.9 %shard_map.85 = (bf16[8,192,128]{2,1,0:T(8,128)(2,1)S(1)}, bf16[8,96,128]{2,1,0:T(8,128)(2,1)S(1)}) custom-call(s32[1,192]{1,0:T(1,128)} %bitcast.1, f32[8]{0:T(128)} %scale_ref.1, bf16[192,512]{1,0:T(8,128)(2,1)} %q_hbm.1, bf16[192,512]{1,0:T(8,128)(2,1)} %k_hbm.1, bf16[192,512]{1,0:T(8,128)(2,1)} %v_hbm.1, bf16[192,512]{1,0:T(8,128)(2,1)} %g_hbm.1), custom_call_target="tpu_custom_call" | custom-call | tf_op jit(solution)/shard_map/pallas_call | solution.py:314
  46.5 1.0 %shard_map.86 = (bf16[192,512]{1,0:T(8,128)(2,1)}, bf16[192,512]{1,0:T(8,128)(2,1)}, bf16[192,512]{1,0:T(8,128)(2,1)}) custom-call(bf16[8,192,128]{2,1,0:T(8,128)(2,1)S(1)} %get-tuple-element.5.kq_ref, bf16[8,96,128]{2,1,0:T(8,128)(2,1)S(1)} %get-tuple-element.6.v_ref), custom_call_target="tpu_custom_call" | custom-call | tf_op jit(solution)/shard_map/pallas_call | solution.py:336
